TPU v7x, 32 devices: a whole 2x2x4 slice. The times are simulated.
32 devices in a mesh: leaf: 4 (over y, core), row: 2 (over x), col: 4 (over z).
Axes of the slice: x: 2, y: 2, z: 4, core: 2. Of those that a mesh axis runs over, the one named last changes fastest.
Arguments:
- child_fronts: float32 [8192, 16384], P('col', ('leaf', 'row')), as said below
- arrow_entries: float32 [128, 16384], P(None, ('leaf', 'row')), as said below
- arrow_pattern: int32 [1, 127], replicated, may hold values 0 or 1
- child_maps: int32 [2, 63], replicated, may hold values from 0 to 125, as said below
Outputs:
- child_factored: float32 [8192, 16384], P('col', ('leaf', 'row'))
- root_front: float32 [16384, 16384], P('col', ('leaf', 'row'))
Inputs may be any that keep to these rules, and one draw needn't show every extreme that they name: child_maps[k, i] is 2 i or 2 i + 1. `child_fronts`: each child front is symmetric and positive definite. The first 128 columns of arrow_entries form a symmetric positive definite matrix.
All inputs are finite; a program needn't handle non-finite values.
Results may differ from a plain program's by a relative error of at most 0.0001.
Values sent between devices are 32-bit elements; how exact they have to be, the bound alone decides.
A program may use at most 320 MiB of HBM per device.

v0:
```python
import jax
import jax.numpy as jnp
from jax import lax
from jax.sharding import PartitionSpec as P

BLK = 128
NB0 = 128
NB1 = 64
SB = 1
UB = 63


def broadcast(value, axis, source):
    kept = jnp.where(lax.axis_index(axis) == source, value, 0).astype(value.dtype)
    return lax.psum(kept, axis)


def from_behind(x, axis, by):
    length = lax.axis_size(axis)
    pairs = [(i, i + by) for i in range(length) if 0 <= i + by < length]
    return lax.ppermute(x, axis, pairs)


def factor_front(front_part, fronts, column_rank, row_rank):
    rows_here, columns_here = front_part.shape
    leaf_count = lax.axis_size("leaf")
    row_count = lax.axis_size("row")
    column_count = lax.axis_size("col")
    per_front = leaf_count * row_count // fronts
    front_index = row_rank // per_front
    row_inner = row_rank - front_index * per_front
    first_index = column_rank * rows_here + jnp.arange(rows_here)
    second_index = row_inner * columns_here + jnp.arange(columns_here)
    leaves = leaf_count // fronts
    source_leaf = column_rank * leaves // column_count
    leaf_width = row_count * columns_here
    first_column = column_rank * rows_here - source_leaf * leaf_width
    front_slots = jnp.arange(fronts) == front_index
    finish = BLK
    owner_column = 0 // rows_here
    owner_row = 0 // columns_here
    row_offset = 0 - owner_column * rows_here
    column_offset = 0 - owner_row * columns_here
    on_column = column_rank == owner_column
    on_both = jnp.logical_and(on_column, row_inner == owner_row)
    diagonal_block = front_part[row_offset : row_offset + BLK, column_offset : column_offset + BLK]
    stacked = jnp.where(
        jnp.logical_and(front_slots, on_both)[:, None, None], diagonal_block[None], 0.0
    )
    summed = lax.psum(stacked, ("leaf", "row"))
    pivot_square = jnp.sum(jnp.where(front_slots[:, None, None], summed, 0.0), axis=0)
    pivot_square = jnp.where(on_column, pivot_square, jnp.eye(BLK, dtype=jnp.float32))
    lower_factor = jnp.linalg.cholesky(pivot_square)
    solved = jax.scipy.linalg.solve_triangular(
        lower_factor, front_part[row_offset : row_offset + BLK, :], lower=True
    )
    upper_mask = second_index[None, :] >= (0 + jnp.arange(BLK))[:, None]
    solved = jnp.where(upper_mask, solved, 0.0)
    own_rows = broadcast(solved, "col", owner_column)
    chosen = jnp.zeros_like(own_rows)
    for front_each in range(fronts):
        copied = broadcast(own_rows, "leaf", front_each * leaves + source_leaf)
        chosen = jnp.where(front_index == front_each, copied, chosen)
    leaf_block = lax.all_gather(chosen, "row", axis=1, tiled=True)
    column_rows = lax.dynamic_slice_in_dim(leaf_block, first_column, rows_here, 1)
    product = lax.dot_general(
        column_rows,
        own_rows,
        (((0,), (0,)), ((), ())),
        precision=lax.Precision.HIGHEST,
        preferred_element_type=jnp.float32,
    )
    trailing = jnp.logical_and(first_index[:, None] >= finish, second_index[None, :] >= finish)
    front_part = jnp.where(trailing, front_part - product, front_part)
    in_block = jnp.logical_and(second_index[None, :] >= 0, second_index[None, :] < finish)
    cleared = jnp.logical_and(first_index[:, None] >= finish, in_block)
    front_part = jnp.where(cleared, 0.0, front_part)
    placed = lax.dynamic_update_slice_in_dim(front_part, own_rows, row_offset, 0)
    in_pivot = jnp.logical_and(first_index >= 0, first_index < finish)
    front_part = jnp.where(in_pivot[:, None], placed, front_part)
    return front_part


def local(child_fronts, arrow_entries, arrow_pattern, child_maps):
    column_rank = lax.axis_index("col")
    row_rank = lax.axis_index(("leaf", "row"))
    grid_rows = lax.axis_size(("leaf", "row"))
    child_result = factor_front(child_fronts, 2, column_rank, row_rank)
    width_here = child_result.shape[0]
    blocks_here = width_here // BLK
    child_columns = child_result.shape[1]
    head_rows = SB * BLK
    update_index = column_rank * blocks_here + jnp.arange(blocks_here)
    valid_rows = update_index < UB
    selector = jnp.arange(UB)[None, :] == update_index[:, None]
    maps_here = jnp.sum(jnp.where(selector[None], child_maps[:, None, :], 0), axis=2)
    parent_slot = maps_here - 2 * column_rank * blocks_here
    matches = parent_slot[:, :, None] == jnp.arange(2 * blocks_here)[None, None, :]
    expansion = jnp.logical_and(matches, valid_rows[None, :, None]).astype(jnp.float32)
    row_table = (child_maps[:, :, None] == jnp.arange(NB0)[None, None, :]).astype(jnp.float32)
    item_rows = lax.all_to_all(
        child_result.reshape(grid_rows, -1, child_columns),
        ("leaf", "row"),
        split_axis=0,
        concat_axis=2,
        tiled=True,
    )
    item_count = item_rows.shape[1]
    update_parts = item_rows.reshape(item_count, 2, NB1, BLK)[:, :, SB:, :]
    mapped = jnp.einsum("mkib,kip->mkpb", update_parts, row_table, precision=lax.Precision.HIGHEST)
    kept_apart = mapped.reshape(1, item_count, 2, NB0 * BLK)
    kept_apart = kept_apart.reshape(-1, 2, NB0 * BLK)
    returned = lax.all_to_all(kept_apart, ("leaf", "row"), split_axis=2, concat_axis=0, tiled=True)
    moved_rows = from_behind(returned[:head_rows], "col", -1)
    shifted = jnp.concatenate([returned[head_rows:], moved_rows], axis=0)
    parent = jnp.einsum(
        "ibkr,kip->pbr",
        shifted.reshape(blocks_here, BLK, 2, -1),
        expansion,
        precision=lax.Precision.HIGHEST,
    )
    parent = parent.reshape(2 * width_here, -1)
    parent_height = parent.shape[0]
    parent_columns = parent.shape[1]
    column_blocks = parent_columns // BLK
    full_pattern = jnp.concatenate([jnp.ones((SB, SB), jnp.int32), arrow_pattern], axis=1)
    pattern_here = lax.dynamic_slice_in_dim(
        full_pattern, row_rank * column_blocks, column_blocks, 1
    )
    keep_mask = jnp.broadcast_to(
        pattern_here[:, None, :, None], (SB, BLK, column_blocks, BLK)
    ).reshape(head_rows, parent_columns)
    masked = jnp.where(keep_mask > 0, arrow_entries, 0.0)
    padded = jnp.concatenate(
        [masked, jnp.zeros((parent_height - head_rows, parent_columns), jnp.float32)], axis=0
    )
    parent = jnp.where(column_rank == 0, parent + padded, parent)
    root_result = factor_front(parent, 1, column_rank, row_rank)
    return (child_result, root_result)


def solution(mesh):
    placed = (P("col", ("leaf", "row")), P(None, ("leaf", "row")), P(), P())
    return jax.shard_map(
        local,
        mesh=mesh,
        in_specs=placed,
        out_specs=(P("col", ("leaf", "row")), P("col", ("leaf", "row"))),
        check_vma=False,
    )
```

profile of v0, /device:TPU:0, one launch (start us, length us, event | category | flops | bytes accessed | tf_op | source)
XLA Modules:
  0.0 1423.5 jit_solution(18297894485424468721)
XLA Ops:
  7.3 0.8 slice.33
  8.9 58.3 %all-reduce.9.cloned.1.call-done = f32[2,128,128]{2,1,0:T(8,128)} async-done(((f32[2,128,128]{2,1,0:T(8,128)}), f32[2,128,128]{2,1,0:T(8,128)}) %all-reduce.9.cloned.1.call-update) | async-done | bytes 131088 | tf_op jit(solution)/shard_map/psum | solution.py:50
  67.3 1.0 select_reduce_fusion
  68.5 11.7 cholesky.44
  81.5 9.8 custom-call.6
  91.4 4.2 fusion.3
  95.6 51.3 %all-reduce.11.cloned.1.call-done = f32[128,2048]{0,1:T(8,128)} async-done(((f32[128,2048]{0,1:T(8,128)}), f32[128,2048]{0,1:T(8,128)}) %all-reduce.11.cloned.1.call-update) | async-done | bytes 1048592 | tf_op jit(solution)/shard_map/psum | solution.py:15
  146.9 2.7 broadcast_select_fusion.2
  149.7 51.3 %all-reduce.19.cloned.1.call-done = (f32[128,2048]{0,1:T(8,128)}, f32[128,2048]{0,1:T(8,128)}) async-done(((f32[128,2048]{0,1:T(8,128)}, f32[128,2048]{0,1:T(8,128)}), (f32[128,2048]{0,1:T(8,128)}, f32[128,2048]{0,1:T(8,128)})) %all-reduce.19.cloned.1.call-update) | async-done | bytes 2097168 | tf_op jit(solution)/shard_map/psum | solution.py:15
  200.9 2.3 select_select_fusion
  203.5 17.9 %copy.71 = f32[2048,2048]{0,1:T(8,128)} copy(f32[2048,2048]{1,0:T(8,128)} %param.7) | data formatting | bytes 33554432 | tf_op args[0]
  222.0 14.6 %all-gather.3.cloned.1.call-done = f32[128,4096]{0,1:T(8,128)} async-done(((f32[128,2048]{0,1:T(8,128)}), f32[128,4096]{0,1:T(8,128)}) %all-gather.3.cloned.1.call-update) | async-done | bytes 2097168 | tf_op jit(solution)/shard_map/all_gather | solution.py:64
  236.6 19.6 %fusion.1 = f32[2048,2048]{0,1:T(8,128)S(1)} fusion(f32[2048,2048]{0,1:T(8,128)} %copy.71, f32[128,2048]{0,1:T(8,128)S(1)} %copy-done.3, pred[2048]{0:T(1024)(128)(4,1)S(1)} %add_compare_fusion.1, pred[2048]{0:T(1024)(128)(4,1)S(1)} %get-tuple-element.18, pred[2048]{0:T(1024)(128)(4,1)S(1)} %get-tuple-element.19, ...), kind=kOutput, calls=%fused_computation.6 | convolution fusion | flops 6463422464 | bytes 35657732 | tf_op jit(solution)/shard_map/dot_general | solution.py:66
  256.2 1.0 fusion.6
  257.2 1.8 copy.102
  258.9 4.1 copy-done
  263.0 186.1 %all_to_all.33 = f32[8,256,2048]{1,2,0:T(8,128)S(1)} all-to-all(f32[8,256,2048]{1,2,0:T(8,128)S(1)} %bitcast.80), channel_id=1, replica_groups=mesh['leaf'=4,'row'=2,'col'=4] {'leaf','row'}, dimensions={0} | all-to-all | bytes 33554432 | tf_op jit(solution)/shard_map/all_to_all | solution.py:101
  449.2 6.2 slice.40
  455.4 16.2 %copy.97 = f32[256,2,63,128]{3,2,0,1:T(8,128)} copy(f32[256,2,63,128]{0,3,2,1:T(8,128)} %slice.40) | data formatting | bytes 33030144
  471.6 23.0 %convolution_bitcast_fusion = f32[256,2,128,128]{3,2,0,1:T(8,128)} fusion(f32[256,2,63,128]{3,2,0,1:T(8,128)} %copy.97, s32[2,63]{1,0:T(2,128)S(1)} %copy-done.5), kind=kOutput, calls=%fused_computation.5 | convolution fusion | flops 6341804032 | bytes 50070008 | tf_op jit(solution)/shard_map/mkib,kip->mkpb/dot_general | solution.py:110
  494.6 38.6 %copy.94 = f32[256,2,128,128]{0,1,3,2:T(2,128)} copy(f32[256,2,128,128]{3,2,0,1:T(8,128)} %convolution_bitcast_fusion) | data formatting | bytes 67108864 | tf_op jit(solution)/shard_map/reshape;reshape | solution.py:112
  533.2 368.3 %all_to_all.34 = f32[256,2,16384]{0,1,2:T(2,128)S(1)} all-to-all(f32[256,2,16384]{0,1,2:T(2,128)} %bitcast.78), channel_id=1, replica_groups=mesh['leaf'=4,'row'=2,'col'=4] {'leaf','row'}, dimensions={2} | all-to-all | bytes 67108864 | tf_op jit(solution)/shard_map/all_to_all | solution.py:113
  901.5 15.1 %copy.77 = f32[256,2,16384]{0,2,1:T(8,128)} copy(f32[256,2,16384]{0,1,2:T(2,128)S(1)} %all_to_all.34) | data formatting | bytes 67108864 | tf_op jit(solution)/shard_map/all_to_all | solution.py:113
  916.7 32.2 %copy.78 = f32[8,256,2,2048]{3,1,0,2:T(8,128)} copy(f32[8,256,2,2048]{1,3,0,2:T(8,128)} %bitcast.79) | data formatting | bytes 67108864 | tf_op jit(solution)/shard_map/all_to_all | solution.py:113
  948.9 3.1 slice.42
  952.0 1.3 collective-permute-start
  954.6 22.2 %slice.41 = f32[1920,2,2048]{2,0,1:T(8,128)} slice(f32[2048,2,2048]{2,0,1:T(8,128)} %bitcast.76), slice={[128:2048], [0:2], [0:2048]} | slice | bytes 62914560 | tf_op jit(solution)/shard_map/slice | solution.py:115
  976.7 25.1 %collective-permute-done = f32[128,2,2048]{2,0,1:T(8,128)} collective-permute-done((f32[128,2,2048]{2,0,1:T(8,128)}, f32[128,2,2048]{2,0,1:T(8,128)}, u32[]{:S(2)}, u32[]{:S(2)}) %collective-permute-start) | collective-permute-done | bytes 2097184 | tf_op jit(solution)/shard_map/ppermute | solution.py:21
  1001.8 23.2 %pad_maximum_fusion = f32[2048,2,2048]{2,0,1:T(8,128)} fusion(f32[128,2,2048]{2,0,1:T(8,128)} %collective-permute-done, f32[1920,2,2048]{2,0,1:T(8,128)} %slice.41), kind=kLoop, calls=%fused_computation.3 | loop fusion | flops 8388608 | bytes 67108864 | tf_op jit(solution)/shard_map/concatenate | solution.py:115
  1025.1 34.6 %copy.90 = f32[16,128,2,2048]{1,0,2,3:T(8,128)} copy(f32[16,128,2,2048]{3,1,0,2:T(8,128)} %bitcast.77) | data formatting | bytes 67108864 | tf_op jit(solution)/shard_map/reshape | solution.py:118
  1059.7 28.7 %fusion.21 = f32[32,128,2048,1]{1,0,3,2:T(8,128)} fusion(f32[16,128,2,2048]{1,0,2,3:T(8,128)} %copy.90, pred[2,16,32,1]{2,1,0,3:T(8,128)(4,1)S(1)} %fusion.44), kind=kOutput, calls=%fused_computation.56 | convolution fusion | flops 3221225472 | bytes 67109888 | tf_op jit(solution)/shard_map/ibkr,kip->pbr/dot_general | solution.py:116
  1088.3 35.7 %add_select_fusion = f32[4096,2048]{0,1:T(8,128)S(1)} fusion(f32[256,8,32,128]{3,2,1,0:T(8,128)} %bitcast.74, f32[128,2048]{0,1:T(8,128)S(1)} %broadcast_select_fusion.1, pred[]{:T(512)S(6)} %eq.98), kind=kLoop, calls=%fused_computation.1 | loop fusion | flops 16777216 | bytes 68157440 | tf_op jit(solution)/shard_map/jit(_where)/select_n | solution.py:137
  1124.0 11.7 copy-done.1
  1136.6 50.8 %all-reduce.13.cloned.1.call-done = f32[1,128,128]{1,2,0:T(8,128)} async-done(((f32[1,128,128]{1,2,0:T(8,128)}), f32[1,128,128]{1,2,0:T(8,128)}) %all-reduce.13.cloned.1.call-update) | async-done | bytes 65552 | tf_op jit(solution)/shard_map/psum | solution.py:50
  1187.4 0.9 convert_select_fusion
  1188.4 0.9 fusion.13
  1189.2 11.7 cholesky.55
  1202.3 9.8 custom-call.7
  1212.1 3.2 fusion.2
  1215.4 51.3 %all-reduce.15.cloned.1.call-done = f32[128,2048]{0,1:T(8,128)} async-done(((f32[128,2048]{0,1:T(8,128)}), f32[128,2048]{0,1:T(8,128)}) %all-reduce.15.cloned.1.call-update) | async-done | bytes 1048592 | tf_op jit(solution)/shard_map/psum | solution.py:15
  1266.7 2.3 broadcast_select_fusion.4
  1269.2 36.0 %all-reduce.17.cloned.1.call-done = f32[128,2048]{0,1:T(8,128)} async-done(((f32[128,2048]{0,1:T(8,128)}), f32[128,2048]{0,1:T(8,128)}) %all-reduce.17.cloned.1.call-update) | async-done | bytes 1048592 | tf_op jit(solution)/shard_map/psum | solution.py:15
  1305.2 2.3 broadcast_select_fusion
  1307.6 17.8 %copy.85 = f32[2048,2048]{1,0:T(8,128)} copy(f32[2048,2048]{0,1:T(8,128)} %copy-done) | data formatting | bytes 33554432
  1325.4 15.7 %all-gather.5.cloned.1.call-done = f32[128,4096]{0,1:T(8,128)} async-done(((f32[128,2048]{0,1:T(8,128)}), f32[128,4096]{0,1:T(8,128)}) %all-gather.5.cloned.1.call-update) | async-done | bytes 2097168 | tf_op jit(solution)/shard_map/all_gather | solution.py:64
  1341.2 39.7 %fusion = f32[4096,2048]{0,1:T(8,128)} fusion(f32[4096,2048]{0,1:T(8,128)} %copy-done.1, pred[4096]{0:T(1024)(128)(4,1)S(1)} %add_compare_fusion, pred[2048]{0:T(1024)(128)(4,1)S(1)} %get-tuple-element.20, pred[2048]{0:T(1024)(128)(4,1)S(1)} %get-tuple-element.21, f32[128,4096]{0,1:T(8,128)} %all-gather.5.cloned.1.call-done, f32[128,2048]{0,1:T(8,128)S(1)} %copy-done.2), kind=kOutput, calls=%fused_computation.2 | convolution fusion | flops 12926844928 | bytes 70262784 | tf_op jit(solution)/shard_map/dot_general | solution.py:66
  1380.8 2.3 fusion.4
  1383.1 33.3 %copy.86 = f32[4096,2048]{1,0:T(8,128)} copy(f32[4096,2048]{0,1:T(8,128)} %fusion.4) | data formatting | bytes 67108864
  (62 shorter events, 7.3 us)
Async XLA Ops:
  7.2 60.1 %all-reduce.9.cloned.1.call-start = ((), (), s32[]{:S(2)}) async-start(), calls=%async_computation.2 | async-start | bytes 262144 | tf_op jit(solution)/shard_map/psum | solution.py:50
  8.9 138.0 %all-reduce.11.cloned.1.call-start = ((), (), s32[]{:S(2)}) async-start(), calls=%async_computation.3 | async-start | bytes 2097152 | tf_op jit(solution)/shard_map/psum | solution.py:15
  95.6 105.4 %all-reduce.19.cloned.1.call-start = ((), (), s32[]{:S(2)}) async-start(), calls=%async_computation.9 | async-start | bytes 4194304 | tf_op jit(solution)/shard_map/psum | solution.py:15
  149.6 87.0 %all-gather.3.cloned.1.call-start = ((), (), s32[]{:S(2)}) async-start(), calls=%async_computation.4 | async-start | bytes 3145728 | tf_op jit(solution)/shard_map/all_gather | solution.py:64
  203.2 984.2 %all-reduce.13.cloned.1.call-start = ((), (), s32[]{:S(2)}) async-start(), calls=%async_computation.5 | async-start | bytes 131072 | tf_op jit(solution)/shard_map/psum | solution.py:50
  203.5 33.1 %copy-start.3 = (f32[128,2048]{0,1:T(8,128)S(1)}, f32[128,2048]{0,1:T(8,128)}, u32[]{:S(2)}) copy-start(f32[128,2048]{0,1:T(8,128)} %all-reduce.11.cloned.1.call-done) | copy-start | bytes 3145732
  257.2 5.9 copy-start
  455.4 16.2 %copy-start.5 = (s32[2,63]{1,0:T(2,128)S(1)}, s32[2,63]{1,0:T(2,128)}, u32[]{:S(2)}) copy-start(s32[2,63]{1,0:T(2,128)} %param.10) | copy-start | bytes 1516
  916.7 36.6 %copy-start.4 = (f32[128,2048]{1,0:T(8,128)S(1)}, f32[128,2048]{1,0:T(8,128)}, u32[]{:S(2)}) copy-start(f32[128,2048]{1,0:T(8,128)} %param.8) | copy-start | bytes 3145732
  916.7 37.0 %copy-start.6 = (s32[1,127]{1,0:T(1,128)S(1)}, s32[1,127]{1,0:T(1,128)}, u32[]{:S(2)}) copy-start(s32[1,127]{1,0:T(1,128)} %param.9) | copy-start | bytes 1528
  952.0 49.8 %collective-permute-start = (f32[128,2,2048]{2,0,1:T(8,128)}, f32[128,2,2048]{2,0,1:T(8,128)}, u32[]{:S(2)}, u32[]{:S(2)}) collective-permute-start(f32[128,2,2048]{2,0,1:T(8,128)} %slice.42), channel_id=1, source_target_pairs={{1,0},{2,1},{3,2},{5,4},{6,5},{7,6},{9,8},{10,9},{11,10},{13,12},{... | collective-permute-start | bytes 6291464 | tf_op jit(solution)/shard_map/ppermute | solution.py:21
  1124.0 11.7 copy-start.1
  1136.4 130.3 %all-reduce.15.cloned.1.call-start = ((), (), s32[]{:S(2)}) async-start(), calls=%async_computation.6 | async-start | bytes 2097152 | tf_op jit(solution)/shard_map/psum | solution.py:15
  1215.3 89.9 %all-reduce.17.cloned.1.call-start = ((), (), s32[]{:S(2)}) async-start(), calls=%async_computation.7 | async-start | bytes 2097152 | tf_op jit(solution)/shard_map/psum | solution.py:15
  1268.9 72.2 %all-gather.5.cloned.1.call-start = ((), (), s32[]{:S(2)}) async-start(), calls=%async_computation.8 | async-start | bytes 3145728 | tf_op jit(solution)/shard_map/all_gather | solution.py:64
  1307.6 33.6 %copy-start.2 = (f32[128,2048]{0,1:T(8,128)S(1)}, f32[128,2048]{0,1:T(8,128)}, u32[]{:S(2)}) copy-start(f32[128,2048]{0,1:T(8,128)} %all-reduce.15.cloned.1.call-done) | copy-start | bytes 3145732
Sparse Core Ops, SparseCore 0:
  11.6 55.6 all-reduce.8
  95.7 51.1 all-reduce.10
  149.9 50.9 all-reduce.18
  203.4 33.1 all-gather.2
  1136.5 50.8 all-reduce.12
  1215.4 51.1 all-reduce.14
  1269.7 35.4 all-reduce.16
  1307.6 33.4 all-gather.4
where the time goes:
time: 1430 us; the launch traced here: 1420 us
  blocking collectives  554 us (39%)
  waiting for transfers between devices  354 us (25%)
  local copies, waits for them, and re-layouts  256 us (18%)
  other arithmetic  123 us (9%)
  matrix products  118 us (8%)
  between operations  14.8 us (1%)
    all_to_all x1, blocking collectives, local(): lax.all_to_all(kept_apart, ('leaf', 'row'), split_axis=2, concat_axis=0,...  368 us
    psum x4, waiting for transfers between devices, broadcast(): return lax.psum(kept, axis)  190 us
    all_to_all x1, blocking collectives, local(): lax.all_to_all(child_result.reshape(grid_rows, -1, child_columns), ('leaf...  186 us
    psum x2, waiting for transfers between devices, factor_front(): summed = lax.psum(stacked, ('leaf', 'row'))  109 us
    unnamed x19, local copies, waits for them, and re-layouts  101 us
    dot_general x2, matrix products, factor_front(): lax.dot_general(column_rows, own_rows, (((0,), (0,)), ((), ())), precisio...  59.3 us
    all_to_all x2, local copies, waits for them, and re-layouts, local(): lax.all_to_all(kept_apart, ('leaf', 'row'), split_axis=2, concat_axis=0,...  47.3 us
    another operation x1, local copies, waits for them, and re-layouts, local(): kept_apart = kept_apart.reshape(-1, 2, NB0 * BLK)  38.6 us
  transfers between devices with their start and end apart: 9, of which 9 were waited for; matrix products, arithmetic and copies ran while one was open for 4% of the time, Pallas kernels for 0%

commit v1 on v0

v1 whole, which is shorter than its diff:
```python
import functools

import jax
import jax.numpy as jnp
from jax import lax
from jax.experimental import pallas as pl
from jax.experimental.pallas import tpu as pltpu
from jax.sharding import PartitionSpec as P

BLK = 128
UB = 63
PLANE = ("leaf", "row")
ALL = ("leaf", "row", "col")
HIGHEST = lax.Precision.HIGHEST


def split_two(x):
    high = lax.reduce_precision(x, 8, 7)
    return high.astype(jnp.bfloat16), (x - high).astype(jnp.bfloat16)


def left_terms(x):
    high, low = split_two(x)
    return jnp.concatenate([high, high, low, low], axis=-1)


def right_terms(x):
    high, low = split_two(x)
    return jnp.concatenate([high, low, high, low], axis=-2)


def factor(diagonal):
    lower = jnp.linalg.cholesky(diagonal)
    eye = jnp.broadcast_to(jnp.eye(BLK, dtype=jnp.float32), diagonal.shape)
    return jax.scipy.linalg.solve_triangular(lower, eye, lower=True)


def dot(a, b, contract):
    return lax.dot_general(
        a, b, (contract, ((), ())), precision=HIGHEST, preferred_element_type=jnp.float32
    )


def root_kernel(
    steps, half, scal, rpar, cpar, win_a, win_b, edge_a, edge_b, next_a, next_b, next_ea, next_eb,
    ur_a, ur_b, uc_a, uc_b, upr, upc, upf, out,
):
    i = pl.program_id(0)
    odd, first_col, first_row = scal[0], scal[1], scal[2]
    width = out.shape[1]
    chunk = min(512, width)
    for n in range(width // chunk):
        part = slice(n * chunk, (n + 1) * chunk)
        out[:, part] = -jnp.dot(upr[...], upc[:, part], preferred_element_type=jnp.float32)
    last = i == steps - 1
    slots = (
        (win_a, edge_a, next_a, next_ea, ur_a, uc_a),
        (win_b, edge_b, next_b, next_eb, ur_b, uc_b),
    )
    for e, (win, edge, nwin, nedge, ur, uc) in enumerate(slots):
        rows = pl.ds(pl.multiple_of(rpar[e * steps + i] * BLK, BLK), BLK)
        for j in range(half):
            product = jnp.dot(
                ur[...], uc[:, j * BLK : (j + 1) * BLK], preferred_element_type=jnp.float32
            )
            if j < half - 1:
                take = pl.ds(pl.multiple_of((j + odd) * BLK, BLK), BLK)
                entry = jnp.where(last, nwin[:, take], win[:, take])
            else:
                take = pl.ds(j * BLK, BLK)
                plain = jnp.where(last, nwin[:, take], win[:, take])
                entry = jnp.where(odd == 1, jnp.where(last, nedge[...], edge[...]), plain)
            cols = pl.ds(pl.multiple_of((2 * j + cpar[e * half + j]) * BLK, BLK), BLK)
            out[rows, cols] += entry - product

    @pl.when(first_row == 1)
    def _():
        out[:, :BLK] = jnp.zeros((2 * BLK, BLK), jnp.float32)

    @pl.when(jnp.logical_and(first_col == 1, i == 0))
    def _():
        out[:BLK, :] = upf[...]


def local(child, arrow, arrow_pattern, child_maps):
    H, W = child.shape
    c = lax.axis_index("col")
    s = lax.axis_index(PLANE)
    G = lax.axis_size(PLANE)
    NC = lax.axis_size("col")
    pf = G // 2
    k = s // pf
    q = s - k * pf
    rb, half = H // BLK, W // BLK // 2
    odd = s % 2
    HW = half * BLK
    PH = 2 * H

    to_a = [(p, 2 * (p % pf) + p // pf) for p in range(G)]
    to_b = [(p, 2 * (p % pf) + 1 - p // pf) for p in range(G)]
    edge_0 = [(p, 2 * p - 1) for p in range(1, pf)]
    edge_1 = [(pf + p, 2 * p - 1) for p in range(1, pf)]

    def route(x):
        left = lax.slice_in_dim(x, BLK, BLK + HW, axis=1)
        start_a = jnp.where(k == 0, BLK, HW)
        start_b = jnp.where(k == 0, HW, BLK)
        del left
        a = lax.ppermute(lax.dynamic_slice_in_dim(x, start_a, HW, 1), PLANE, to_a)
        b = lax.ppermute(lax.dynamic_slice_in_dim(x, start_b, HW, 1), PLANE, to_b)
        ea = lax.ppermute(x[:, :BLK], PLANE, edge_1)
        eb = lax.ppermute(x[:, :BLK], PLANE, edge_0)
        return a, b, ea, eb

    on_col = c == 0
    kids = jnp.arange(2)
    head = jnp.where(jnp.logical_and(on_col, q == 0), child[:BLK, :BLK], 0.0)
    diagonals = lax.psum(jnp.where((kids == k)[:, None, None], head[None], 0.0), ALL)
    raw_cols = lax.psum(jnp.where(on_col, child[:BLK, :], 0.0), "col")
    own_edge = jnp.where(q == 0, child[:, :BLK], 0.0)
    raw_rows = lax.psum(jnp.where((kids == k)[:, None, None], own_edge[None], 0.0), PLANE)
    back = [(p + 1, p) for p in range(NC - 1)]
    below = lax.ppermute(child[:BLK, :], "col", back)
    rows_below = lax.ppermute(raw_rows[:, :BLK], "col", back)

    bulk_a, bulk_b, bulk_ea, bulk_eb = route(child)

    inverses = factor(diagonals)
    own_inverse = jnp.where(k == 0, inverses[0], inverses[1])
    second_index = q * W + jnp.arange(W)
    upper = second_index[None, :] >= jnp.arange(BLK)[:, None]
    u_cols = jnp.where(upper, dot(own_inverse, raw_cols, ((1,), (0,))), 0.0)
    raw_ext = jnp.concatenate([raw_rows, rows_below], axis=1)
    u_rows = jnp.stack([dot(raw_ext[e], inverses[e], ((1,), (1,))) for e in range(2)])
    own_rows = jnp.where(k == 0, u_rows[0, :H], u_rows[1, :H])
    second_block = child[BLK : 2 * BLK, :] - dot(own_rows[BLK : 2 * BLK], u_cols, ((1,), (0,)))

    small = jnp.concatenate([u_cols, second_block, below], axis=0)
    small_a, small_b, small_ea, small_eb = route(small)

    def aligned(win, edge):
        shifted = jnp.concatenate([win, edge], axis=1)
        return jnp.where(odd == 1, shifted[:, BLK:], win)

    heads = [aligned(w[: 2 * BLK], e[: 2 * BLK]) for w, e in ((small_a, small_ea), (small_b, small_eb))]

    maps = jnp.concatenate([child_maps % 2, jnp.zeros((2, G * half - UB), jnp.int32)], axis=1)
    maps = jnp.where(odd == 1, maps[::-1], maps)
    row_par = lax.dynamic_slice_in_dim(maps, c * rb, rb, 1)
    col_par = lax.dynamic_slice_in_dim(maps, s * half, half, 1)

    full_pattern = jnp.concatenate([jnp.ones((1, 1), jnp.int32), arrow_pattern], axis=1)
    pattern_here = lax.dynamic_slice_in_dim(full_pattern, s * 2 * half, 2 * half, 1)
    keep = jnp.repeat(pattern_here, BLK, axis=1)
    pivot = jnp.where(keep > 0, arrow, 0.0)
    for e in range(2):
        given = heads[e][BLK:]
        pieces = []
        for j in range(half):
            block = given[:, j * BLK : (j + 1) * BLK]
            for a in range(2):
                here = jnp.logical_and(maps[e, 0] == 0, col_par[e, j] == a)
                pieces.append(jnp.where(here, block, 0.0))
        pivot = pivot + jnp.concatenate(pieces, axis=1)
    pivot = jnp.where(on_col, pivot, 0.0)
    root_diagonal = lax.psum(
        jnp.where(s == 0, pivot[:, :BLK], 0.0), ALL
    )
    pivot_cols = lax.psum(pivot, "col")
    sources = PH // W
    place = jnp.arange(sources) == s - sources * c
    pivot_rows = lax.psum(jnp.where(place[:, None, None], pivot_cols[None], 0.0), PLANE)
    root_inverse = factor(root_diagonal)
    root_index = s * W + jnp.arange(W)
    root_upper = root_index[None, :] >= jnp.arange(BLK)[:, None]
    up_cols = jnp.where(root_upper, dot(root_inverse, pivot_cols, ((1,), (0,))), 0.0)
    up_rows = jnp.concatenate(
        [dot(pivot_rows[e], root_inverse, ((0,), (1,))) for e in range(sources)], axis=0
    )

    first_index = c * H + jnp.arange(H)
    product = dot(own_rows, u_cols, ((1,), (0,)))
    trailing = jnp.logical_and(first_index[:, None] >= BLK, second_index[None, :] >= BLK)
    child_result = jnp.where(trailing, child - product, 0.0)
    child_result = child_result.at[:BLK].set(jnp.where(on_col, u_cols, child_result[:BLK]))

    slot_rows = jnp.where(odd == 1, u_rows[::-1], u_rows)[:, BLK:]
    scal = jnp.stack([odd, on_col.astype(jnp.int32), (s == 0).astype(jnp.int32)]).astype(jnp.int32)
    down = lambda i, *_: (jnp.minimum(i + 1, rb - 1), 0)
    fixed = lambda i, *_: (0, 0)
    step = lambda i, *_: (i, 0)
    in_specs = [
        pl.BlockSpec((BLK, HW), down),
        pl.BlockSpec((BLK, HW), down),
        pl.BlockSpec((BLK, BLK), down),
        pl.BlockSpec((BLK, BLK), down),
        pl.BlockSpec((BLK, HW), fixed),
        pl.BlockSpec((BLK, HW), fixed),
        pl.BlockSpec((BLK, BLK), fixed),
        pl.BlockSpec((BLK, BLK), fixed),
        pl.BlockSpec((BLK, 4 * BLK), step),
        pl.BlockSpec((BLK, 4 * BLK), step),
        pl.BlockSpec((4 * BLK, HW), fixed),
        pl.BlockSpec((4 * BLK, HW), fixed),
        pl.BlockSpec((2 * BLK, 4 * BLK), step),
        pl.BlockSpec((4 * BLK, W), fixed),
        pl.BlockSpec((BLK, W), fixed),
    ]
    root_result = pl.pallas_call(
        functools.partial(root_kernel, rb, half),
        out_shape=jax.ShapeDtypeStruct((PH, W), jnp.float32),
        grid_spec=pltpu.PrefetchScalarGridSpec(
            num_scalar_prefetch=3,
            grid=(rb,),
            in_specs=in_specs,
            out_specs=pl.BlockSpec((2 * BLK, W), step),
        ),
        compiler_params=pltpu.CompilerParams(vmem_limit_bytes=40 << 20),
        name="root_front",
    )(
        scal, row_par.reshape(-1), col_par.reshape(-1),
        bulk_a, bulk_b, bulk_ea, bulk_eb,
        small_a[2 * BLK :], small_b[2 * BLK :], small_ea[2 * BLK :], small_eb[2 * BLK :],
        left_terms(slot_rows[0]), left_terms(slot_rows[1]),
        right_terms(heads[0][:BLK]), right_terms(heads[1][:BLK]),
        left_terms(up_rows), right_terms(up_cols), up_cols,
    )
    return child_result, root_result


def solution(mesh):
    placed = (P("col", PLANE), P(None, PLANE), P(), P())
    return jax.shard_map(
        local,
        mesh=mesh,
        in_specs=placed,
        out_specs=(P("col", PLANE), P("col", PLANE)),
        check_vma=False,
    )
```

time: 1430 us -> 809 us (0.57)
  blocking collectives: 554 us -> 0 us
  local copies, waits for them, and re-layouts: 256 us -> 25.3 us
  waiting for transfers between devices: 354 us -> 501 us
  matrix products: 118 us -> 33.7 us
  starting transfers between devices: 2.21 us -> 75.2 us
  Pallas kernels: 0 us -> 31.5 us
  other arithmetic: 123 us -> 99.4 us
  between operations: 14.8 us -> 36.4 us
    all_to_all x2 -> x0, blocking collectives: 554 us -> none  [the longest x1 368 us: local(): lax.all_to_all(kept_apart, ('leaf', 'row'), split_axis=2, concat_axis=0,...]
    psum x6, waiting for transfers between devices: 299 us -> 501 us  [the longest x1 260 us: local(): root_diagonal = lax.psum(jnp.where(s == 0, pivot[:, :BLK], 0.0), ALL)]
    unnamed x19 -> x47, local copies, waits for them, and re-layouts: 101 us -> 3.81 us
    dot_general x4 -> x8, matrix products: 111 us -> 33.1 us  [dot(): lax.dot_general(a, b, (contract, ((), ())), precision=HIGHEST, preferred_...]
    ppermute x1 -> x10, starting transfers between devices: 1.28 us -> 74.8 us  [the longest x2 65.2 us: route(): a = lax.ppermute(lax.dynamic_slice_in_dim(x, start_a, HW, 1), PLANE, to_a)]
    all_to_all x2 -> x0, local copies, waits for them, and re-layouts: 47.3 us -> none  [local(): lax.all_to_all(kept_apart, ('leaf', 'row'), split_axis=2, concat_axis=0,...]
    select_n x14 -> x12, other arithmetic: 51.7 us -> 7.41 us  [the longest x1 2.89 us: local(): jnp.where(place[:, None, None], pivot_cols[None], 0.0)]
    another operation x1 -> x0, local copies, waits for them, and re-layouts: 38.6 us -> none  [local(): kept_apart = kept_apart.reshape(-1, 2, NB0 * BLK)]
  transfers between devices with their start and end apart: 9 -> 16, of which waited for: 9 -> 6; matrix products, arithmetic and copies ran while one was open for 4% -> 19% of each run, Pallas kernels for 0% -> 0%
where the time goes in v1:
time: 809 us; the launch traced here: 803 us
  waiting for transfers between devices  501 us (62%)
  other arithmetic  99.4 us (12%)
  starting transfers between devices  75.2 us (9%)
  between operations  36.4 us (4%)
  matrix products  33.7 us (4%)
  Pallas kernels  31.5 us (4%)
  local copies, waits for them, and re-layouts  25.3 us (3%)
    psum x1, waiting for transfers between devices, local(): root_diagonal = lax.psum(jnp.where(s == 0, pivot[:, :BLK], 0.0), ALL)  260 us
    psum x1, waiting for transfers between devices, local(): lax.psum(jnp.where((kids == k)[:, None, None], head[None], 0.0), ALL)  84.1 us
    ppermute x2, starting transfers between devices, route(): a = lax.ppermute(lax.dynamic_slice_in_dim(x, start_a, HW, 1), PLANE, to_a)  65.2 us
    psum x1, waiting for transfers between devices, local(): raw_cols = lax.psum(jnp.where(on_col, child[:BLK, :], 0.0), 'col')  50.9 us
    psum x1, waiting for transfers between devices, local(): lax.psum(jnp.where(place[:, None, None], pivot_cols[None], 0.0), PLANE)  45.9 us
    psum x1, waiting for transfers between devices, local(): pivot_cols = lax.psum(pivot, 'col')  41.5 us
    another operation x7, other arithmetic, factor(): lower = jnp.linalg.cholesky(diagonal)  36 us
    dot_general x8, matrix products, dot(): lax.dot_general(a, b, (contract, ((), ())), precision=HIGHEST, preferred_...  33.1 us
  transfers between devices with their start and end apart: 16, of which 6 were waited for; matrix products, arithmetic and copies ran while one was open for 19% of the time, Pallas kernels for 0%

profile of v1, /device:TPU:0, one launch (start us, length us, event | category | flops | bytes accessed | tf_op | source)
XLA Modules:
  0.0 802.8 jit_solution(12394863835162142301)
XLA Ops:
  7.3 0.8 slice_select_fusion.3
  8.9 2.3 fusion.25
  11.2 1.5 broadcast_select_fusion.1
  12.9 1.6 collective-permute-start.3
  14.5 1.6 collective-permute-start.4
  16.1 2.4 fusion.24
  18.5 1.3 collective-permute-start.5
  24.4 11.1 %constant_dynamic-slice_fusion.3 = (f32[2048,1024]{1,0:T(8,128)}, f32[2048,1024]{1,0:T(8,128)}) fusion(f32[2048,2048]{1,0:T(8,128)} %param.6, s32[]{:T(128)S(6)} %select_n.378, s32[]{:T(128)S(6)} %select_n.377), kind=kLoop, calls=%fused_computation.126 | loop fusion | bytes 33554440 | tf_op jit(solution)/shard_map/dynamic_slice | solution.py:110
  57.2 84.1 %all-reduce.10.cloned.1.call-done = f32[2,128,128]{2,1,0:T(8,128)} async-done(((f32[2,128,128]{2,1,0:T(8,128)}), f32[2,128,128]{2,1,0:T(8,128)}) %all-reduce.10.cloned.1.call-update) | async-done | bytes 131088 | tf_op jit(solution)/shard_map/psum | solution.py:118
  141.2 1.0 copy.11
  142.2 0.9 fusion.14
  143.2 23.5 %custom-call.15 = f32[2,128,128]{2,1,0:T(8,128)S(1)} custom-call(f32[2,128,128]{2,1,0:T(8,128)S(1)} %fusion.14), custom_call_target="Cholesky" | custom-call | tf_op jit(solution)/shard_map/jit(cholesky)/cholesky | solution.py:33
  166.9 19.7 %custom-call.16 = f32[2,1,128,128]{2,3,1,0:T(8,128)S(1)} custom-call(f32[2,1,128,128]{3,2,1,0:T(8,128)S(1)} %select_bitcast_fusion), custom_call_target="InvertDiagBlocksLowerTriangular" | custom-call | tf_op jit(solution)/shard_map/jit(_solve_triangular)/vmap()/triangular_solve | solution.py:35
  186.9 19.0 %all-reduce.8.cloned.1.call-done = f32[2,2048,128]{2,1,0:T(8,128)} async-done(((f32[2,2048,128]{2,1,0:T(8,128)}), f32[2,2048,128]{2,1,0:T(8,128)}) %all-reduce.8.cloned.1.call-update) | async-done | bytes 2097168 | tf_op jit(solution)/shard_map/psum | solution.py:121
  206.0 1.1 slice.378
  207.1 1.5 collective-permute-start
  208.5 50.9 %all-reduce.12.cloned.1.call-done = f32[128,2048]{1,0:T(8,128)} async-done(((f32[128,2048]{1,0:T(8,128)}), f32[128,2048]{1,0:T(8,128)}) %all-reduce.12.cloned.1.call-update) | async-done | bytes 1048592 | tf_op jit(solution)/shard_map/psum | solution.py:119
  259.4 2.3 convolution_select_fusion.1
  261.8 1.0 convolution_bitcast_fusion.1
  262.9 1.0 convolution_bitcast_fusion
  264.1 2.2 convolution_subtract_fusion
  266.3 1.7 pad_maximum_fusion.1
  269.9 2.2 collective-permute-start.7
  272.3 1.5 reduce-precision_convert_fusion.2
  273.8 19.2 %subtract_select_fusion = f32[2048,2048]{1,0:T(8,128)} fusion(f32[2048,2048]{1,0:T(8,128)} %param.6, f32[128,2048]{1,0:T(8,128)S(1)} %convolution_select_fusion.1, pred[2048]{0:T(1024)(128)(4,1)S(1)} %copy-done.18, pred[2048]{0:T(1024)(128)(4,1)S(1)} %copy-done.19, f32[1,2048,128]{2,1,0:T(8,128)S(1)} %slice_select_fusion.1), kind=kOutput, calls=%fused_computation | convolution fusion | flops 6455033856 | bytes 35655680 | tf_op jit(solution)/shard_map/dot_general | solution.py:39
  293.0 2.3 fusion.8
  295.3 64.4 %collective-permute-start.1 = (f32[2048,1024]{1,0:T(8,128)}, f32[2048,1024]{1,0:T(8,128)}, u32[]{:S(2)}, u32[]{:S(2)}) collective-permute-start(f32[2048,1024]{1,0:T(8,128)} %get-tuple-element.19), channel_id=1, source_target_pairs={{0,0},{4,8},{8,16},{12,24},{16,4},{20,12},{24,20},{28,28},{1,1},{5... | collective-permute-start | bytes 25165832 | tf_op jit(solution)/shard_map/ppermute | solution.py:109
  364.7 3.6 pad_maximum_fusion.3
  368.4 0.8 slice.391.next_eb
  369.5 2.0 slice.387.next_a
  371.5 1.9 slice.388.next_b
  373.5 1.1 pad_maximum_fusion.10.uc_b
  374.7 1.1 pad_maximum_fusion.9.uc_a
  375.8 259.8 %all-reduce.18.cloned.1.call-done = f32[128,128]{1,0:T(8,128)} async-done(((f32[128,128]{1,0:T(8,128)}), f32[128,128]{1,0:T(8,128)}) %all-reduce.18.cloned.1.call-update) | async-done | bytes 65552 | tf_op jit(solution)/shard_map/psum | solution.py:166
  635.6 0.9 copy.15
  636.5 0.9 fusion.18
  637.4 11.7 %cholesky.60 = f32[128,128]{1,0:T(8,128)S(1)} custom-call(f32[128,128]{1,0:T(8,128)S(1)} %fusion.18), custom_call_target="Cholesky" | custom-call | tf_op jit(solution)/shard_map/jit(cholesky)/cholesky | solution.py:33
  649.1 41.5 %all-reduce.14.cloned.1.call-done = f32[128,2048]{1,0:T(8,128)} async-done(((f32[128,2048]{1,0:T(8,128)}), f32[128,2048]{1,0:T(8,128)}) %all-reduce.14.cloned.1.call-update) | async-done | bytes 1048592 | tf_op jit(solution)/shard_map/psum | solution.py:169
  690.6 2.9 broadcast_select_fusion
  694.8 9.8 %custom-call.17 = f32[1,128,128]{1,2,0:T(8,128)S(1)} custom-call(f32[1,128,128]{2,1,0:T(8,128)S(1)} %fusion.15), custom_call_target="InvertDiagBlocksLowerTriangular" | custom-call | tf_op jit(solution)/shard_map/jit(_solve_triangular)/triangular_solve | solution.py:35
  704.8 2.4 reduce-precision_convert_fusion.1
  707.2 1.6 pad_maximum_fusion.6.upc
  708.8 45.9 %all-reduce.16.cloned.1.call-done = f32[2,128,2048]{2,1,0:T(8,128)} async-done(((f32[2,128,2048]{2,1,0:T(8,128)}), f32[2,128,2048]{2,1,0:T(8,128)}) %all-reduce.16.cloned.1.call-update) | async-done | bytes 2097168 | tf_op jit(solution)/shard_map/psum | solution.py:172
  754.7 3.2 fusion.5
  757.9 1.8 fusion.4
  760.1 2.3 pad_maximum_fusion.upr
  762.7 1.1 copy-done.1
  764.4 31.5 %root_front.1 = f32[4096,2048]{1,0:T(8,128)} custom-call(s32[3]{0:T(128)S(1)} %pad_add_fusion.scal, s32[32]{0:T(128)S(1)} %reshape.205.rpar, s32[16]{0:T(128)S(1)} %reshape.206.cpar, f32[2048,1024]{1,0:T(8,128)} %collective-permute-done.1.win_a, f32[2048,1024]{1,0:T(8,128)} %collective-permute-done.2.win_b, f32[2048,128]{1,0:T(8,128)} %collective-permute-done.3.edge_a, ...), custom_call_target="tpu_custom_call" | custom-call | tf_op jit(solution)/shard_map/root_front/pallas_call | solution.py:209
  (154 shorter events, 16.5 us)
Async XLA Ops:
  7.2 134.1 %all-reduce.10.cloned.1.call-start = ((), (), s32[]{:S(2)}) async-start(), calls=%async_computation.1 | async-start | bytes 262144 | tf_op jit(solution)/shard_map/psum | solution.py:118
  8.9 197.1 %all-reduce.8.cloned.1.call-start = ((), (), s32[]{:S(2)}) async-start(), calls=%async_computation | async-start | bytes 4194304 | tf_op jit(solution)/shard_map/psum | solution.py:121
  12.8 8.3 %copy-start.20 = (s32[2,63]{1,0:T(2,128)S(1)}, s32[2,63]{1,0:T(2,128)}, u32[]{:S(2)}) copy-start(s32[2,63]{1,0:T(2,128)} %param.9) | copy-start | bytes 1516
  12.8 9.7 %copy-start.22 = (s32[1,127]{1,0:T(1,128)S(1)}, s32[1,127]{1,0:T(1,128)}, u32[]{:S(2)}) copy-start(s32[1,127]{1,0:T(1,128)} %param.8) | copy-start | bytes 1528
  12.8 246.6 %all-reduce.12.cloned.1.call-start = ((), (), s32[]{:S(2)}) async-start(), calls=%async_computation.2 | async-start | bytes 2097152 | tf_op jit(solution)/shard_map/psum | solution.py:119
  12.9 749.5 %collective-permute-start.3 = (f32[2048,128]{1,0:T(8,128)}, f32[2048,128]{1,0:T(8,128)}, u32[]{:S(2)}, u32[]{:S(2)}) collective-permute-start(f32[2048,128]{1,0:T(8,128)} %get-tuple-element.16), channel_id=1, source_target_pairs={{20,4},{24,12},{28,20},{21,5},{25,13},{29,21},{22,6},{26,14},{30,2... | collective-permute-start | bytes 3145736 | tf_op jit(solution)/shard_map/ppermute | solution.py:111
  14.5 747.9 %collective-permute-start.4 = (f32[2048,128]{1,0:T(8,128)}, f32[2048,128]{1,0:T(8,128)}, u32[]{:S(2)}, u32[]{:S(2)}) collective-permute-start(f32[2048,128]{1,0:T(8,128)} %get-tuple-element.16), channel_id=1, source_target_pairs={{4,4},{8,12},{12,20},{5,5},{9,13},{13,21},{6,6},{10,14},{14,22},{7... | collective-permute-start | bytes 3145736 | tf_op jit(solution)/shard_map/ppermute | solution.py:112
  18.5 247.8 %collective-permute-start.5 = (f32[128,2048]{1,0:T(8,128)S(1)}, f32[128,2048]{1,0:T(8,128)}, u32[]{:S(2)}, u32[]{:S(2)}) collective-permute-start(f32[128,2048]{1,0:T(8,128)S(1)} %get-tuple-element.14), channel_id=1, source_target_pairs={{1,0},{2,1},{3,2},{5,4},{6,5},{7,6},{9,8},{10,9},{11,10},{13,12},{... | collective-permute-start | bytes 3145736 | tf_op jit(solution)/shard_map/ppermute | solution.py:123
  19.8 615.8 %all-reduce.18.cloned.1.call-start = ((), (), s32[]{:S(2)}) async-start(), calls=%async_computation.5 | async-start | bytes 131072 | tf_op jit(solution)/shard_map/psum | solution.py:166
  206.0 55.7 %copy-start.9 = (f32[2,2048,128]{2,1,0:T(8,128)S(1)}, f32[2,2048,128]{2,1,0:T(8,128)}, u32[]{:S(2)}) copy-start(f32[2,2048,128]{2,1,0:T(8,128)} %all-reduce.8.cloned.1.call-done) | copy-start | bytes 6291460
  207.1 54.8 %collective-permute-start = (f32[2,128,128]{2,1,0:T(8,128)S(1)}, f32[2,128,128]{2,1,0:T(8,128)S(1)}, u32[]{:S(2)}, u32[]{:S(2)}) collective-permute-start(f32[2,128,128]{2,1,0:T(8,128)S(1)} %slice.378), channel_id=1, source_target_pairs={{1,0},{2,1},{3,2},{5,4},{6,5},{7,6},{9,8},{10,9},{11,10},{13,12},{... | collective-permute-start | bytes 393224 | tf_op jit(solution)/shard_map/ppermute | solution.py:124
  268.4 26.8 %collective-permute-start.9 = (f32[384,128]{1,0:T(8,128)S(1)}, f32[384,128]{1,0:T(8,128)S(1)}, u32[]{:S(2)}, u32[]{:S(2)}) collective-permute-start(f32[384,128]{1,0:T(8,128)S(1)} %slice.389), channel_id=1, source_target_pairs={{4,4},{8,12},{12,20},{5,5},{9,13},{13,21},{6,6},{10,14},{14,22},{7... | collective-permute-start | bytes 589832 | tf_op jit(solution)/shard_map/ppermute | solution.py:112
  269.1 90.6 %collective-permute-start.8 = (f32[384,128]{1,0:T(8,128)S(1)}, f32[384,128]{1,0:T(8,128)S(1)}, u32[]{:S(2)}, u32[]{:S(2)}) collective-permute-start(f32[384,128]{1,0:T(8,128)S(1)} %slice.389), channel_id=1, source_target_pairs={{20,4},{24,12},{28,20},{21,5},{25,13},{29,21},{22,6},{26,14},{30,2... | collective-permute-start | bytes 589832 | tf_op jit(solution)/shard_map/ppermute | solution.py:111
  269.9 89.8 %collective-permute-start.7 = (f32[384,1024]{1,0:T(8,128)S(1)}, f32[384,1024]{1,0:T(8,128)S(1)}, u32[]{:S(2)}, u32[]{:S(2)}) collective-permute-start(f32[384,1024]{1,0:T(8,128)S(1)} %get-tuple-element.20), channel_id=1, source_target_pairs={{0,4},{4,12},{8,20},{12,28},{16,0},{20,8},{24,16},{28,24},{1,5},{5... | collective-permute-start | bytes 4718600 | tf_op jit(solution)/shard_map/ppermute | solution.py:110
  272.3 1.5 copy-start.18
  272.3 1.5 copy-start.19
  295.3 65.3 %copy-start.16 = (f32[384,128]{1,0:T(8,128)}, f32[384,128]{1,0:T(8,128)S(1)}, u32[]{:S(2)}) copy-start(f32[384,128]{1,0:T(8,128)S(1)} %collective-permute-done.9) | copy-start | bytes 589828
  295.3 467.1 %collective-permute-start.1 = (f32[2048,1024]{1,0:T(8,128)}, f32[2048,1024]{1,0:T(8,128)}, u32[]{:S(2)}, u32[]{:S(2)}) collective-permute-start(f32[2048,1024]{1,0:T(8,128)} %get-tuple-element.19), channel_id=1, source_target_pairs={{0,0},{4,8},{8,16},{12,24},{16,4},{20,12},{24,20},{28,28},{1,1},{5... | collective-permute-start | bytes 25165832 | tf_op jit(solution)/shard_map/ppermute | solution.py:109
  359.7 1.1 copy-start.14
  359.7 402.7 %collective-permute-start.2 = (f32[2048,1024]{1,0:T(8,128)}, f32[2048,1024]{1,0:T(8,128)}, u32[]{:S(2)}, u32[]{:S(2)}) collective-permute-start(f32[2048,1024]{1,0:T(8,128)} %get-tuple-element.18), channel_id=1, source_target_pairs={{0,4},{4,12},{8,20},{12,28},{16,0},{20,8},{24,16},{28,24},{1,5},{5... | collective-permute-start | bytes 25165832 | tf_op jit(solution)/shard_map/ppermute | solution.py:110
  359.8 1.2 copy-start.11
  359.8 1.5 collective-permute-start.6
  360.8 0.9 slice-start
  361.3 1.1 copy-start.12
  361.7 1.7 copy-start.13
  361.8 1.8 copy-start.6
  363.6 1.0 copy-start.8
  364.4 326.3 %all-reduce.14.cloned.1.call-start = ((), (), s32[]{:S(2)}) async-start(), calls=%async_computation.3 | async-start | bytes 2097152 | tf_op jit(solution)/shard_map/psum | solution.py:169
  364.7 3.6 copy-start.15
  369.2 385.4 %all-reduce.16.cloned.1.call-start = ((), (), s32[]{:S(2)}) async-start(), calls=%async_computation.4 | async-start | bytes 4194304 | tf_op jit(solution)/shard_map/psum | solution.py:172
  369.5 5.1 copy-start.7
  373.5 317.2 %copy-start.21 = (pred[2]{0:T(512)(128)(4,1)S(1)}, pred[2]{0:T(512)(128)(4,1)}, u32[]{:S(2)}) copy-start(pred[2]{0:T(512)(128)(4,1)} %iota_compare_fusion.5) | copy-start | bytes 10
  649.1 55.7 %copy-start.17 = (s32[2048]{0:T(1024)S(1)}, s32[2048]{0:T(1024)}, u32[]{:S(2)}) copy-start(s32[2048]{0:T(1024)} %iota_add_fusion) | copy-start | bytes 24580
  754.7 3.2 copy-start.10
  759.7 2.7 copy-start.4
  759.7 2.7 copy-start.5
  760.0 2.7 copy-start
  760.1 3.8 copy-start.1
  760.1 4.0 copy-start.2
  760.1 4.3 copy-start.3
Sparse Core Ops, SparseCore 0:
  13.5 127.6 all-reduce.9
  145.0 60.9 all-reduce.7
  208.4 50.9 all-reduce.11
  364.5 271.0 all-reduce.17
  637.9 52.6 all-reduce.13
  693.7 60.8 all-reduce.15

commit v2 on v1

--- a/solution.py
+++ b/solution.py
@@ -102,10 +102,8 @@
     edge_1 = [(pf + p, 2 * p - 1) for p in range(1, pf)]
 
     def route(x):
-        left = lax.slice_in_dim(x, BLK, BLK + HW, axis=1)
         start_a = jnp.where(k == 0, BLK, HW)
         start_b = jnp.where(k == 0, HW, BLK)
-        del left
         a = lax.ppermute(lax.dynamic_slice_in_dim(x, start_a, HW, 1), PLANE, to_a)
         b = lax.ppermute(lax.dynamic_slice_in_dim(x, start_b, HW, 1), PLANE, to_b)
         ea = lax.ppermute(x[:, :BLK], PLANE, edge_1)
@@ -114,26 +112,32 @@
 
     on_col = c == 0
     kids = jnp.arange(2)
-    head = jnp.where(jnp.logical_and(on_col, q == 0), child[:BLK, :BLK], 0.0)
+    head = jnp.where(jnp.logical_and(on_col, q == 0), child[:BLK, : 2 * BLK], 0.0)
     diagonals = lax.psum(jnp.where((kids == k)[:, None, None], head[None], 0.0), ALL)
-    raw_cols = lax.psum(jnp.where(on_col, child[:BLK, :], 0.0), "col")
+    raw_cols = lax.psum(jnp.where(on_col, child[: 2 * BLK, :], 0.0), "col")
     own_edge = jnp.where(q == 0, child[:, :BLK], 0.0)
     raw_rows = lax.psum(jnp.where((kids == k)[:, None, None], own_edge[None], 0.0), PLANE)
     back = [(p + 1, p) for p in range(NC - 1)]
     below = lax.ppermute(child[:BLK, :], "col", back)
     rows_below = lax.ppermute(raw_rows[:, :BLK], "col", back)
 
-    bulk_a, bulk_b, bulk_ea, bulk_eb = route(child)
-
-    inverses = factor(diagonals)
+    bulk = route(child)
+    bulk, raw_cols, raw_rows, rows_below, below = lax.optimization_barrier(
+        (bulk, raw_cols, raw_rows, rows_below, below)
+    )
+    bulk_a, bulk_b, bulk_ea, bulk_eb = bulk
+
+    inverses = factor(diagonals[:, :, :BLK])
     own_inverse = jnp.where(k == 0, inverses[0], inverses[1])
     second_index = q * W + jnp.arange(W)
     upper = second_index[None, :] >= jnp.arange(BLK)[:, None]
-    u_cols = jnp.where(upper, dot(own_inverse, raw_cols, ((1,), (0,))), 0.0)
+    u_cols = jnp.where(upper, dot(own_inverse, raw_cols[:BLK], ((1,), (0,))), 0.0)
     raw_ext = jnp.concatenate([raw_rows, rows_below], axis=1)
     u_rows = jnp.stack([dot(raw_ext[e], inverses[e], ((1,), (1,))) for e in range(2)])
     own_rows = jnp.where(k == 0, u_rows[0, :H], u_rows[1, :H])
-    second_block = child[BLK : 2 * BLK, :] - dot(own_rows[BLK : 2 * BLK], u_cols, ((1,), (0,)))
+    own_second = jnp.where(k == 0, diagonals[0, :, BLK:], diagonals[1, :, BLK:])
+    u_second = dot(own_inverse, own_second, ((1,), (0,)))
+    second_block = raw_cols[BLK:] - dot(u_second, u_cols, ((0,), (0,)))
 
     small = jnp.concatenate([u_cols, second_block, below], axis=0)
     small_a, small_b, small_ea, small_eb = route(small)
@@ -162,11 +166,8 @@
                 here = jnp.logical_and(maps[e, 0] == 0, col_par[e, j] == a)
                 pieces.append(jnp.where(here, block, 0.0))
         pivot = pivot + jnp.concatenate(pieces, axis=1)
-    pivot = jnp.where(on_col, pivot, 0.0)
-    root_diagonal = lax.psum(
-        jnp.where(s == 0, pivot[:, :BLK], 0.0), ALL
-    )
-    pivot_cols = lax.psum(pivot, "col")
+    root_diagonal = lax.psum(jnp.where(s == 0, pivot[:, :BLK], 0.0), PLANE)
+    pivot_cols = pivot
     sources = PH // W
     place = jnp.arange(sources) == s - sources * c
     pivot_rows = lax.psum(jnp.where(place[:, None, None], pivot_cols[None], 0.0), PLANE)

time: 809 us -> 568 us (0.70)
  waiting for transfers between devices: 501 us -> 264 us
    psum x4 -> x2, waiting for transfers between devices: 398 us -> 135 us  [the longest x1 80.2 us: local(): raw_cols = lax.psum(jnp.where(on_col, child[:2 * BLK, :], 0.0), 'col')]
    ppermute x2, waiting for transfers between devices: 0.01 us -> 10.6 us  [route(): b = lax.ppermute(lax.dynamic_slice_in_dim(x, start_b, HW, 1), PLANE, to_b)]
    psum x1, waiting for transfers between devices: 84.1 us -> 93.8 us  [local(): lax.psum(jnp.where((kids == k)[:, None, None], head[None], 0.0), ALL)]
    dot_general x8 -> x9, matrix products: 33.1 us -> 33.2 us  [dot(): lax.dot_general(a, b, (contract, ((), ())), precision=HIGHEST, preferred_...]
  transfers between devices with their start and end apart: 16 -> 14, of which waited for: 6 -> 6; matrix products, arithmetic and copies ran while one was open for 19% -> 18% of each run, Pallas kernels for 0% -> 0%
where the time goes in v2:
time: 568 us; the launch traced here: 562 us
  waiting for transfers between devices  264 us (46%)
  other arithmetic  93.8 us (17%)
  starting transfers between devices  73.2 us (13%)
  between operations  36 us (6%)
  matrix products  34.7 us (6%)
  Pallas kernels  31.2 us (5%)
  local copies, waits for them, and re-layouts  29.1 us (5%)
    psum x1, waiting for transfers between devices, local(): lax.psum(jnp.where((kids == k)[:, None, None], head[None], 0.0), ALL)  93.8 us
    psum x1, waiting for transfers between devices, local(): raw_cols = lax.psum(jnp.where(on_col, child[:2 * BLK, :], 0.0), 'col')  80.2 us
    ppermute x2, starting transfers between devices, route(): a = lax.ppermute(lax.dynamic_slice_in_dim(x, start_a, HW, 1), PLANE, to_a)  65.1 us
    psum x1, waiting for transfers between devices, local(): root_diagonal = lax.psum(jnp.where(s == 0, pivot[:, :BLK], 0.0), PLANE)  55.1 us
    another operation x7, other arithmetic, factor(): lower = jnp.linalg.cholesky(diagonal)  36 us
    dot_general x9, matrix products, dot(): lax.dot_general(a, b, (contract, ((), ())), precision=HIGHEST, preferred_...  33.2 us
    pallas_call x1, Pallas kernels, local(): pl.pallas_call(functools.partial(root_kernel, rb, half), out_shape=jax.Sh...  31.2 us
    another operation x5, other arithmetic, factor(): return jax.scipy.linalg.solve_triangular(lower, eye, lower=True)  30.8 us
  transfers between devices with their start and end apart: 14, of which 6 were waited for; matrix products, arithmetic and copies ran while one was open for 18% of the time, Pallas kernels for 0%

profile of v2, /device:TPU:0, one launch (start us, length us, event | category | flops | bytes accessed | tf_op | source)
XLA Modules:
  0.0 561.9 jit_solution(13310062203746827180)
XLA Ops:
  7.2 11.1 %constant_dynamic-slice_fusion.5 = (f32[2048,1024]{1,0:T(8,128)}, f32[2048,1024]{1,0:T(8,128)}) fusion(f32[2048,2048]{1,0:T(8,128)} %param.6, s32[]{:T(128)S(6)} %select_n.370, s32[]{:T(128)S(6)} %select_n.369), kind=kLoop, calls=%fused_computation.144 | loop fusion | bytes 33554440 | tf_op jit(solution)/shard_map/dynamic_slice | solution.py:108
  18.3 64.4 %collective-permute-start = (f32[2048,1024]{1,0:T(8,128)}, f32[2048,1024]{1,0:T(8,128)}, u32[]{:S(2)}, u32[]{:S(2)}) collective-permute-start(f32[2048,1024]{1,0:T(8,128)} %get-tuple-element.35), channel_id=1, source_target_pairs={{0,0},{4,8},{8,16},{12,24},{16,4},{20,12},{24,20},{28,28},{1,1},{5... | collective-permute-start | bytes 25165832 | tf_op jit(solution)/shard_map/ppermute | solution.py:107
  82.7 0.9 slice_select_fusion.3
  84.6 1.4 broadcast_select_fusion.2
  85.9 1.6 broadcast_select_fusion.1
  89.1 2.3 slice.323
  91.4 1.4 collective-permute-start.5
  92.8 3.2 slice_select_fusion
  119.4 93.8 %all-reduce.11.cloned.1.call-done = f32[2,128,256]{1,2,0:T(8,128)} async-done(((f32[2,128,256]{1,2,0:T(8,128)}), f32[2,128,256]{1,2,0:T(8,128)}) %all-reduce.11.cloned.1.call-update) | async-done | bytes 262160 | tf_op jit(solution)/shard_map/psum | solution.py:116
  213.3 0.9 slice.391
  214.3 0.9 fusion.18
  215.2 23.5 %custom-call.15 = f32[2,128,128]{2,1,0:T(8,128)S(1)} custom-call(f32[2,128,128]{2,1,0:T(8,128)S(1)} %fusion.18), custom_call_target="Cholesky" | custom-call | tf_op jit(solution)/shard_map/jit(cholesky)/cholesky | solution.py:33
  238.9 20.3 %custom-call.16 = f32[2,1,128,128]{2,3,1,0:T(8,128)} custom-call(f32[2,1,128,128]{3,2,1,0:T(8,128)S(1)} %select_bitcast_fusion), custom_call_target="InvertDiagBlocksLowerTriangular" | custom-call | tf_op jit(solution)/shard_map/jit(_solve_triangular)/vmap()/triangular_solve | solution.py:35
  259.2 1.3 fusion.16
  260.5 19.7 %all-reduce.9.cloned.1.call-done = f32[2,2048,128]{2,1,0:T(8,128)} async-done(((f32[2,2048,128]{2,1,0:T(8,128)}), f32[2,2048,128]{2,1,0:T(8,128)}) %all-reduce.9.cloned.1.call-update) | async-done | bytes 2097168 | tf_op jit(solution)/shard_map/psum | solution.py:119
  280.2 0.9 slice.389
  281.2 1.5 collective-permute-start.4
  282.7 1.2 fusion.21
  283.9 4.3 collective-permute-done.4
  288.1 80.2 %all-reduce.7.cloned.1.call-done = f32[256,2048]{1,0:T(8,128)} async-done(((f32[256,2048]{1,0:T(8,128)}), f32[256,2048]{1,0:T(8,128)}) %all-reduce.7.cloned.1.call-update) | async-done | bytes 2097168 | tf_op jit(solution)/shard_map/psum | solution.py:117
  368.4 2.5 convolution_select_fusion.1
  370.8 1.1 slice_subtract_fusion
  371.9 1.7 pad_maximum_fusion.1
  375.7 0.9 constant_dynamic-update-slice_fusion
  376.6 1.0 convolution_bitcast_fusion.1
  377.7 1.0 convolution_bitcast_fusion
  378.7 2.1 collective-permute-start.7
  381.9 1.5 reduce-precision_convert_fusion.2
  383.5 19.2 %subtract_select_fusion = f32[2048,2048]{1,0:T(8,128)} fusion(f32[2048,2048]{1,0:T(8,128)} %param.6, f32[128,2048]{1,0:T(8,128)S(1)} %convolution_select_fusion.1, pred[2048]{0:T(1024)(128)(4,1)S(1)} %broadcast_compare_fusion, pred[2048]{0:T(1024)(128)(4,1)S(1)} %add_compare_fusion, f32[1,2176,128]{2,1,0:T(8,128)S(1)} %convolution_bitcast_fusion, ...), kind=kOutput, calls=%fused_computation | convolution fusion | flops 6455296000 | bytes 36704256 | tf_op jit(solution)/shard_map/dot_general | solution.py:39
  402.6 2.3 fusion.8
  405.0 10.6 %collective-permute-done.7 = f32[384,1024]{1,0:T(8,128)S(1)} collective-permute-done((f32[384,1024]{1,0:T(8,128)S(1)}, f32[384,1024]{1,0:T(8,128)S(1)}, u32[]{:S(2)}, u32[]{:S(2)}) %collective-permute-start.7) | collective-permute-done | bytes 1572896 | tf_op jit(solution)/shard_map/ppermute | solution.py:108
  415.9 0.9 copy-done.14
  417.4 0.9 copy-done.15
  420.5 1.6 broadcast_select_fusion
  422.1 3.7 pad_maximum_fusion.3
  426.7 2.0 slice.400.next_a
  428.7 1.9 slice.401.next_b
  430.9 1.1 pad_maximum_fusion.9.uc_a
  432.1 55.1 %all-reduce.13.cloned.1.call-done = (f32[128,128]{1,0:T(8,128)}, f32[2,128,2048]{2,1,0:T(8,128)}) async-done(((f32[128,128]{1,0:T(8,128)}, f32[2,128,2048]{2,1,0:T(8,128)}), (f32[128,128]{1,0:T(8,128)}, f32[2,128,2048]{2,1,0:T(8,128)})) %all-reduce.13.cloned.1.call-update) | async-done | bytes 2162704 | tf_op jit(solution)/shard_map/psum | solution.py:169
  487.1 0.9 copy.21
  488.1 0.9 fusion.26
  488.9 11.7 %cholesky.63 = f32[128,128]{1,0:T(8,128)S(1)} custom-call(f32[128,128]{1,0:T(8,128)S(1)} %fusion.26), custom_call_target="Cholesky" | custom-call | tf_op jit(solution)/shard_map/jit(cholesky)/cholesky | solution.py:33
  501.9 9.8 %custom-call.17 = f32[1,128,128]{1,2,0:T(8,128)S(1)} custom-call(f32[1,128,128]{2,1,0:T(8,128)S(1)} %fusion.19), custom_call_target="InvertDiagBlocksLowerTriangular" | custom-call | tf_op jit(solution)/shard_map/jit(_solve_triangular)/triangular_solve | solution.py:35
  512.0 3.1 fusion.5
  515.1 3.0 fusion.4
  518.1 1.2 reduce-precision_convert_fusion.1
  519.9 2.3 pad_maximum_fusion.upr
  524.2 31.2 %root_front.1 = f32[4096,2048]{1,0:T(8,128)} custom-call(s32[3]{0:T(128)S(1)} %pad_add_fusion.scal, s32[32]{0:T(128)S(1)} %reshape.206.rpar, s32[16]{0:T(128)S(1)} %reshape.207.cpar, f32[2048,1024]{1,0:T(8,128)} %collective-permute-done.win_a, f32[2048,1024]{1,0:T(8,128)} %collective-permute-done.1.win_b, f32[2048,128]{1,0:T(8,128)S(1)} %copy-done.5, ...), custom_call_target="tpu_custom_call" | custom-call | tf_op jit(solution)/shard_map/root_front/pallas_call | solution.py:210
  (149 shorter events, 16.0 us)
Async XLA Ops:
  7.2 206.1 %all-reduce.11.cloned.1.call-start = ((), (), s32[]{:S(2)}) async-start(), calls=%async_computation.2 | async-start | bytes 524288 | tf_op jit(solution)/shard_map/psum | solution.py:116
  18.3 350.1 %collective-permute-start = (f32[2048,1024]{1,0:T(8,128)}, f32[2048,1024]{1,0:T(8,128)}, u32[]{:S(2)}, u32[]{:S(2)}) collective-permute-start(f32[2048,1024]{1,0:T(8,128)} %get-tuple-element.35), channel_id=1, source_target_pairs={{0,0},{4,8},{8,16},{12,24},{16,4},{20,12},{24,20},{28,28},{1,1},{5... | collective-permute-start | bytes 25165832 | tf_op jit(solution)/shard_map/ppermute | solution.py:107
  82.7 285.7 %collective-permute-start.1 = (f32[2048,1024]{1,0:T(8,128)}, f32[2048,1024]{1,0:T(8,128)}, u32[]{:S(2)}, u32[]{:S(2)}) collective-permute-start(f32[2048,1024]{1,0:T(8,128)} %get-tuple-element.34), channel_id=1, source_target_pairs={{0,4},{4,12},{8,20},{12,28},{16,0},{20,8},{24,16},{28,24},{1,5},{5... | collective-permute-start | bytes 25165832 | tf_op jit(solution)/shard_map/ppermute | solution.py:108
  84.5 195.7 %all-reduce.9.cloned.1.call-start = ((), (), s32[]{:S(2)}) async-start(), calls=%async_computation.1 | async-start | bytes 4194304 | tf_op jit(solution)/shard_map/psum | solution.py:119
  87.6 280.8 %all-reduce.7.cloned.1.call-start = ((), (), s32[]{:S(2)}) async-start(), calls=%async_computation | async-start | bytes 4194304 | tf_op jit(solution)/shard_map/psum | solution.py:117
  87.6 193.5 %collective-permute-start.2 = (f32[2048,128]{1,0:T(8,128)S(1)}, f32[2048,128]{1,0:T(8,128)S(1)}, u32[]{:S(2)}, u32[]{:S(2)}) collective-permute-start(f32[2048,128]{1,0:T(8,128)S(1)} %get-tuple-element.33), channel_id=1, source_target_pairs={{20,4},{24,12},{28,20},{21,5},{25,13},{29,21},{22,6},{26,14},{30,2... | collective-permute-start | bytes 3145736 | tf_op jit(solution)/shard_map/ppermute | solution.py:109
  88.4 195.5 %collective-permute-start.3 = (f32[2048,128]{1,0:T(8,128)S(1)}, f32[2048,128]{1,0:T(8,128)S(1)}, u32[]{:S(2)}, u32[]{:S(2)}) collective-permute-start(f32[2048,128]{1,0:T(8,128)S(1)} %get-tuple-element.33), channel_id=1, source_target_pairs={{4,4},{8,12},{12,20},{5,5},{9,13},{13,21},{6,6},{10,14},{14,22},{7... | collective-permute-start | bytes 3145736 | tf_op jit(solution)/shard_map/ppermute | solution.py:110
  91.4 4.7 copy-start.20
  91.4 4.8 copy-start.21
  91.4 192.4 %collective-permute-start.5 = (f32[128,2048]{1,0:T(8,128)}, f32[128,2048]{1,0:T(8,128)}, u32[]{:S(2)}, u32[]{:S(2)}) collective-permute-start(f32[128,2048]{1,0:T(8,128)} %slice.323), channel_id=1, source_target_pairs={{1,0},{2,1},{3,2},{5,4},{6,5},{7,6},{9,8},{10,9},{11,10},{13,12},{... | collective-permute-start | bytes 3145736 | tf_op jit(solution)/shard_map/ppermute | solution.py:121
  96.1 391.1 %all-reduce.13.cloned.1.call-start = ((), (), s32[]{:S(2)}) async-start(), calls=%async_computation.3 | async-start | bytes 4325376 | tf_op jit(solution)/shard_map/psum | solution.py:169
  281.2 90.7 %copy-start.4 = (f32[2048,128]{1,0:T(8,128)}, f32[2048,128]{1,0:T(8,128)S(1)}, u32[]{:S(2)}) copy-start(f32[2048,128]{1,0:T(8,128)S(1)} %collective-permute-done.2.edge_a) | copy-start | bytes 3145732
  281.2 7.0 %collective-permute-start.4 = (f32[2,128,128]{2,1,0:T(8,128)S(1)}, f32[2,128,128]{2,1,0:T(8,128)}, u32[]{:S(2)}, u32[]{:S(2)}) collective-permute-start(f32[2,128,128]{2,1,0:T(8,128)S(1)} %slice.389), channel_id=1, source_target_pairs={{1,0},{2,1},{3,2},{5,4},{6,5},{7,6},{9,8},{10,9},{11,10},{13,12},{... | collective-permute-start | bytes 393224 | tf_op jit(solution)/shard_map/ppermute | solution.py:122
  283.8 88.1 %copy-start.6 = (f32[2048,128]{1,0:T(8,128)}, f32[2048,128]{1,0:T(8,128)S(1)}, u32[]{:S(2)}) copy-start(f32[2048,128]{1,0:T(8,128)S(1)} %collective-permute-done.3.edge_b) | copy-start | bytes 3145732
  368.4 2.5 copy-start.13
  373.6 1.9 copy-start.12
  374.0 30.9 %collective-permute-start.9 = (f32[384,128]{1,0:T(8,128)S(1)}, f32[384,128]{1,0:T(8,128)S(1)}, u32[]{:S(2)}, u32[]{:S(2)}) collective-permute-start(f32[384,128]{1,0:T(8,128)S(1)} %slice.402), channel_id=1, source_target_pairs={{4,4},{8,12},{12,20},{5,5},{9,13},{13,21},{6,6},{10,14},{14,22},{7... | collective-permute-start | bytes 589832 | tf_op jit(solution)/shard_map/ppermute | solution.py:110
  374.9 30.1 %collective-permute-start.8 = (f32[384,128]{1,0:T(8,128)S(1)}, f32[384,128]{1,0:T(8,128)S(1)}, u32[]{:S(2)}, u32[]{:S(2)}) collective-permute-start(f32[384,128]{1,0:T(8,128)S(1)} %slice.402), channel_id=1, source_target_pairs={{20,4},{24,12},{28,20},{21,5},{25,13},{29,21},{22,6},{26,14},{30,2... | collective-permute-start | bytes 589832 | tf_op jit(solution)/shard_map/ppermute | solution.py:109
  378.7 36.9 %collective-permute-start.7 = (f32[384,1024]{1,0:T(8,128)S(1)}, f32[384,1024]{1,0:T(8,128)S(1)}, u32[]{:S(2)}, u32[]{:S(2)}) collective-permute-start(f32[384,1024]{1,0:T(8,128)S(1)} %get-tuple-element.36), channel_id=1, source_target_pairs={{0,4},{4,12},{8,20},{12,28},{16,0},{20,8},{24,16},{28,24},{1,5},{5... | collective-permute-start | bytes 4718600 | tf_op jit(solution)/shard_map/ppermute | solution.py:108
  380.9 36.3 %collective-permute-start.6 = (f32[384,1024]{1,0:T(8,128)S(1)}, f32[384,1024]{1,0:T(8,128)S(1)}, u32[]{:S(2)}, u32[]{:S(2)}) collective-permute-start(f32[384,1024]{1,0:T(8,128)S(1)} %get-tuple-element.37), channel_id=1, source_target_pairs={{0,0},{4,8},{8,16},{12,24},{16,4},{20,12},{24,20},{28,28},{1,1},{5... | collective-permute-start | bytes 4718600 | tf_op jit(solution)/shard_map/ppermute | solution.py:107
  405.0 10.7 %copy-start.19 = (f32[384,128]{1,0:T(8,128)}, f32[384,128]{1,0:T(8,128)S(1)}, u32[]{:S(2)}) copy-start(f32[384,128]{1,0:T(8,128)S(1)} %collective-permute-done.9) | copy-start | bytes 589828
  405.0 10.9 %copy-start.17 = (f32[384,128]{1,0:T(8,128)}, f32[384,128]{1,0:T(8,128)S(1)}, u32[]{:S(2)}) copy-start(f32[384,128]{1,0:T(8,128)S(1)} %collective-permute-done.8) | copy-start | bytes 589828
  415.6 1.2 copy-start.14
  415.9 1.4 slice-start
  417.1 1.1 copy-start.15
  417.2 2.0 copy-start.16
  417.4 1.2 copy-start.10
  419.5 1.0 copy-start.8
  422.1 3.7 copy-start.18
  426.7 4.1 copy-start.11
  511.7 6.4 %copy-start.9 = (f32[128,2048]{1,0:T(8,128)S(1)}, f32[128,2048]{1,0:T(8,128)}, u32[]{:S(2)}) copy-start(f32[128,2048]{1,0:T(8,128)} %copy-done.8) | copy-start | bytes 3145732
  519.9 2.5 copy-start
  519.9 3.4 copy-start.1
  519.9 3.5 copy-start.2
  519.9 3.6 copy-start.3
  519.9 4.0 copy-start.5
  519.9 4.3 copy-start.7
Sparse Core Ops, SparseCore 0:
  84.6 128.5 all-reduce.10
  216.5 63.6 all-reduce.8
  282.6 85.7 all-reduce.6
  422.2 64.8 all-reduce.12
